TPU v7x, 32 devices: a whole 2x2x4 slice. The times are simulated.
32 devices in a mesh: row: 4 (over y, x), col: 8 (over z, core).
Axes of the slice: x: 2, y: 2, z: 4, core: 2. Of those that a mesh axis runs over, the one named last changes fastest.
Arguments:
- out_grad: bfloat16 [4096, 8192], P('row', 'col'), may hold values from -0.059814453 to 0.059814453
- hidden: bfloat16 [4096, 28672], P('row', 'col'), may hold values from -6 to 6
- basis: bfloat16 [8192, 1024], P('col'), may hold values from -0.0625 to 0.0625
- weight: bfloat16 [8192, 28672], P('row', 'col'), may hold values from -6 to 6
- first_moment: float32 [1024, 28672], P('row', 'col'), may hold values from -4 to 4
- second_moment: float32 [1024, 28672], P('row', 'col'), may hold values from 0.25 to 4
Outputs:
- new_weight: bfloat16 [8192, 28672], P('row', 'col')
- new_first: float32 [1024, 28672], P('row', 'col')
- new_second: float32 [1024, 28672], P('row', 'col')
All inputs are finite; a program needn't handle non-finite values.
Results may differ from a plain program's by a relative error of at most 0.0039.
Values may be sent and summed in bfloat16 or wider, within the bound.
A program may use at most 128 MiB of HBM per device.

v0:
```python
import jax
import jax.numpy as jnp
from jax import lax
from jax.sharding import PartitionSpec as P

STEP_COUNT = 1000
beta_one = 0.9
beta_two = 0.999
epsilon = 1e-08
step_size = 1.0


def spread(block, axis, source):
    block = jnp.where(lax.axis_index(axis) == source, block, jnp.zeros_like(block))
    return lax.psum(block, axis)


def local(out_grad, hidden, basis, weight, first_moment, second_moment):
    partial_value = jnp.dot(out_grad, basis, preferred_element_type=jnp.float32)
    projected = lax.psum(partial_value, "col").astype(jnp.bfloat16)
    columns = projected
    gradient = lax.psum_scatter(
        lax.dot_general(
            columns, hidden, (((0,), (0,)), ((), ())), preferred_element_type=jnp.float32
        ).astype(jnp.bfloat16),
        "row",
        scatter_dimension=0,
        tiled=True,
    ).astype(jnp.float32)
    new_first = beta_one * first_moment + (1.0 - beta_one) * gradient
    new_second = beta_two * second_moment + (1.0 - beta_two) * gradient * gradient
    first_hat = new_first / (1.0 - beta_one**STEP_COUNT)
    second_hat = new_second / (1.0 - beta_two**STEP_COUNT)
    direction = (first_hat / (jnp.sqrt(second_hat) + epsilon)).astype(jnp.bfloat16)
    per_band = lax.axis_size("col") // lax.axis_size("row")
    blocks = [
        spread(basis, "col", lax.axis_index("row") * per_band + offset)
        for offset in range(per_band)
    ]
    local_basis = jnp.concatenate(blocks, 0)
    initial = jnp.zeros((local_basis.shape[0], direction.shape[1]), jnp.float32)
    portion = lax.all_gather(direction, "row", axis=0, tiled=True)
    columns = lax.slice_in_dim(local_basis, 0, portion.shape[0], axis=1)
    update = initial + jnp.dot(columns, portion, preferred_element_type=jnp.float32)
    new_weight = (weight.astype(jnp.float32) - step_size * update).astype(jnp.bfloat16)
    return (new_weight, new_first, new_second)


def solution(mesh):
    in_specs = (
        P("row", "col"),
        P("row", "col"),
        P("col", None),
        P("row", "col"),
        P("row", "col"),
        P("row", "col"),
    )
    out_specs = (P("row", "col"), P("row", "col"), P("row", "col"))
    return jax.shard_map(local, mesh=mesh, in_specs=in_specs, out_specs=out_specs, check_vma=False)
```

profile of v0, /device:TPU:0, one launch (start us, length us, event | category | flops | bytes accessed | tf_op | source)
XLA Modules:
  0.0 316.9 jit_solution(15711441214757857168)
XLA Ops:
  8.0 0.0 copy-start
  8.0 0.0 reduce-scatter.2.cloned.1.call-start
  8.1 1.5 copy-done
  9.6 5.9 %fusion.9 = f32[1024,1024]{1,0:T(8,128)} fusion(bf16[1024,1024]{1,0:T(8,128)(2,1)S(1)} %copy-done, bf16[1024,1024]{1,0:T(8,128)(2,1)} %param.8), kind=kOutput, calls=%fused_computation.14 | convolution fusion | flops 2147483648 | bytes 8388608 | tf_op jit(solution)/shard_map/dot_general | solution.py:19
  15.5 90.6 %all-reduce.5 = bf16[1024,1024]{1,0:T(8,128)(2,1)S(1)} all-reduce(f32[1024,1024]{1,0:T(8,128)} %fusion.9), channel_id=1, replica_groups=mesh['row'=4,'col'=8] {'col'}, use_global_device_ids=true, to_apply=%region_2.3 | all-reduce | flops 1048576 | bytes 6291456 | tf_op jit(solution)/shard_map/psum | solution.py:20
  106.1 13.0 %convolution_convert_fusion = bf16[1024,3584]{1,0:T(8,128)(2,1)} fusion(bf16[1024,3584]{1,0:T(8,128)(2,1)} %param.7, bf16[1024,1024]{1,0:T(8,128)(2,1)S(1)} %all-reduce.5), kind=kOutput, calls=%fused_computation.1 | convolution fusion | flops 7519862784 | bytes 16777216 | tf_op jit(solution)/shard_map/dot_general | solution.py:23
  119.1 0.0 copy-start.2
  119.1 0.0 reduce-scatter.2.cloned.1.call-update
  119.1 0.0 all-reduce.4.cloned.1.call-start
  119.2 1.5 copy-done.2
  120.7 2.3 broadcast_select_fusion.1
  123.0 0.0 all-reduce.4.cloned.1.call-update
  123.0 0.2 all-gather.2.cloned.1.call-start
  123.3 74.2 %reduce-scatter.2.cloned.1.call-done = bf16[256,3584]{1,0:T(8,128)(2,1)} async-done(((bf16[1024,3584]{1,0:T(8,128)(2,1)}), bf16[256,3584]{1,0:T(8,128)(2,1)}) %reduce-scatter.2.cloned.1.call-update) | async-done | bytes 1835024 | tf_op jit(solution)/shard_map/reduce_scatter | solution.py:22
  197.5 8.8 %divide_convert_fusion = (bf16[256,3584]{1,0:T(8,128)(2,1)}, f32[256,3584]{1,0:T(8,128)}, f32[256,3584]{1,0:T(8,128)}) fusion(bf16[256,3584]{1,0:T(8,128)(2,1)} %reduce-scatter.2.cloned.1.call-done, f32[256,3584]{1,0:T(8,128)} %param.11, f32[256,3584]{1,0:T(8,128)} %param.10), kind=kLoop, calls=%fused_computation.9 | loop fusion | flops 11010048 | bytes 18350080 | tf_op jit(solution)/shard_map/convert_element_type | solution.py:34
  206.4 0.0 all-gather.2.cloned.1.call-update
  206.4 12.6 %all-reduce.4.cloned.1.call-done = (bf16[1024,1024]{1,0:T(8,128)(2,1)}, bf16[1024,1024]{1,0:T(8,128)(2,1)}) async-done(((bf16[1024,1024]{1,0:T(8,128)(2,1)}, bf16[1024,1024]{1,0:T(8,128)(2,1)}), (bf16[1024,1024]{1,0:T(8,128)(2,1)}, bf16[1024,1024]{1,0:T(8,128)(2,1)})) %all-reduce.4.cloned.1.call-update) | async-done | bytes 4194320 | tf_op jit(solution)/shard_map/psum | solution.py:15
  219.0 66.3 %all-gather.2.cloned.1.call-done = bf16[1024,3584]{1,0:T(8,128)(2,1)} async-done(((bf16[256,3584]{1,0:T(8,128)(2,1)}), bf16[1024,3584]{1,0:T(8,128)(2,1)}) %all-gather.2.cloned.1.call-update) | async-done | bytes 7340048 | tf_op jit(solution)/shard_map/all_gather | solution.py:42
  285.3 0.0 copy-start.1
  285.3 24.2 %subtract_convert_fusion = bf16[2048,3584]{1,0:T(8,128)(2,1)} fusion(bf16[2048,3584]{1,0:T(8,128)(2,1)} %param.9, bf16[1024,3584]{1,0:T(8,128)(2,1)} %all-gather.2.cloned.1.call-done, bf16[1024,1024]{1,0:T(8,128)(2,1)} %get-tuple-element.3, bf16[1024,1024]{1,0:T(8,128)(2,1)} %get-tuple-element.4), kind=kOutput, calls=%fused_computation | convolution fusion | flops 15062794240 | bytes 40894464 | tf_op jit(solution)/shard_map/dot_general | solution.py:44
  309.5 0.0 copy-done.1
Async XLA Ops:
  8.0 1.6 copy-start
  8.0 189.5 %reduce-scatter.2.cloned.1.call-start = ((), (), s32[]{:S(2)}) async-start(), calls=%async_computation.1 | async-start | bytes 9175040 | tf_op jit(solution)/shard_map/reduce_scatter | solution.py:22
  119.1 1.6 copy-start.2
  119.1 99.9 %all-reduce.4.cloned.1.call-start = ((), (), s32[]{:S(2)}) async-start(), calls=%async_computation.3 | async-start | bytes 8388608 | tf_op jit(solution)/shard_map/psum | solution.py:15
  123.0 162.2 %all-gather.2.cloned.1.call-start = ((), (), s32[]{:S(2)}) async-start(), calls=%async_computation.2 | async-start | bytes 9175040 | tf_op jit(solution)/shard_map/all_gather | solution.py:42
  285.3 24.2 %copy-start.1 = (bf16[1024,1024]{1,0:T(8,128)(2,1)S(1)}, bf16[1024,1024]{1,0:T(8,128)(2,1)}, u32[]{:S(2)}) copy-start(bf16[1024,1024]{1,0:T(8,128)(2,1)} %param.6) | copy-start | bytes 6291460
Sparse Core Ops, SparseCore 0:
  119.3 78.2 reduce-scatter.1
  206.5 78.7 all-gather.1
Sparse Core Ops, SparseCore 1:
  123.1 95.8 all-reduce.3
where the time goes:
time: 317 us
  waiting for transfers between devices  153 us (48%)
  blocking collectives  90.6 us (29%)
  matrix products  43.1 us (14%)
  between operations  15.5 us (5%)
  other arithmetic  11.1 us (4%)
    psum x1, blocking collectives, local(): projected = lax.psum(partial_value, 'col').astype(jnp.bfloat16)  90.6 us
    reduce_scatter x1, waiting for transfers between devices, local(): lax.psum_scatter(lax.dot_general(columns, hidden, (((0,), (0,)), ((), ())...  74.2 us
    all_gather x1, waiting for transfers between devices, local(): portion = lax.all_gather(direction, 'row', axis=0, tiled=True)  66.3 us
    dot_general x1, matrix products, local(): jnp.dot(columns, portion, preferred_element_type=jnp.float32)  24.2 us
    dot_general x1, matrix products, local(): lax.dot_general(columns, hidden, (((0,), (0,)), ((), ())), preferred_elem...  13 us
    psum x1, waiting for transfers between devices, spread(): return lax.psum(block, axis)  12.6 us
    convert_element_type x1, other arithmetic, local(): (first_hat / (jnp.sqrt(second_hat) + epsilon)).astype(jnp.bfloat16)  8.84 us
  transfers between devices with their start and end apart: 3, of which 3 were waited for; matrix products, arithmetic and copies ran while one was open for 4% of the time, Pallas kernels for 0%

commit v1 on v0

--- a/solution.py
+++ b/solution.py
@@ -17,7 +17,7 @@
 
 def local(out_grad, hidden, basis, weight, first_moment, second_moment):
     partial_value = jnp.dot(out_grad, basis, preferred_element_type=jnp.float32)
-    projected = lax.psum(partial_value, "col").astype(jnp.bfloat16)
+    projected = lax.all_gather(partial_value, "col").sum(axis=0).astype(jnp.bfloat16)
     columns = projected
     gradient = lax.psum_scatter(
         lax.dot_general(

time: 317 us -> 620 us (1.96)
  waiting for transfers between devices: 153 us -> 536 us
  blocking collectives: 90.6 us -> 0 us
  other arithmetic: 11.1 us -> 23.9 us
    all_gather x0 -> x1, waiting for transfers between devices: none -> 291 us  [local(): lax.all_gather(partial_value, 'col').sum(axis=0).astype(jnp.bfloat16)]
    psum x1 -> x0, blocking collectives: 90.6 us -> none  [local(): projected = lax.psum(partial_value, 'col').astype(jnp.bfloat16)]
    psum x1, waiting for transfers between devices: 12.6 us -> 90.2 us  [spread(): return lax.psum(block, axis)]
    all_gather x1, waiting for transfers between devices: 66.3 us -> 81.1 us  [local(): portion = lax.all_gather(direction, 'row', axis=0, tiled=True)]
    reduce_sum x0 -> x1, other arithmetic: none -> 12.9 us  [local(): lax.all_gather(partial_value, 'col').sum(axis=0).astype(jnp.bfloat16)]
  transfers between devices with their start and end apart: 3 -> 4, of which waited for: 3 -> 4; matrix products, arithmetic and copies ran while one was open for 4% -> 2% of each run, Pallas kernels for 0% -> 0%
where the time goes in v1:
time: 620 us
  waiting for transfers between devices  536 us (86%)
  matrix products  43.1 us (7%)
  other arithmetic  23.9 us (4%)
  between operations  13.8 us (2%)
    all_gather x1, waiting for transfers between devices, local(): lax.all_gather(partial_value, 'col').sum(axis=0).astype(jnp.bfloat16)  291 us
    psum x1, waiting for transfers between devices, spread(): return lax.psum(block, axis)  90.2 us
    all_gather x1, waiting for transfers between devices, local(): portion = lax.all_gather(direction, 'row', axis=0, tiled=True)  81.1 us
    reduce_scatter x1, waiting for transfers between devices, local(): lax.psum_scatter(lax.dot_general(columns, hidden, (((0,), (0,)), ((), ())...  73 us
    dot_general x1, matrix products, local(): jnp.dot(columns, portion, preferred_element_type=jnp.float32)  24.2 us
    dot_general x1, matrix products, local(): lax.dot_general(columns, hidden, (((0,), (0,)), ((), ())), preferred_elem...  13 us
    reduce_sum x1, other arithmetic, local(): lax.all_gather(partial_value, 'col').sum(axis=0).astype(jnp.bfloat16)  12.9 us
  transfers between devices with their start and end apart: 4, of which 4 were waited for; matrix products, arithmetic and copies ran while one was open for 2% of the time, Pallas kernels for 0%

profile of v1, /device:TPU:0, one launch (start us, length us, event | category | flops | bytes accessed | tf_op | source)
XLA Modules:
  0.0 620.0 jit_solution(4130490073210630273)
XLA Ops:
  7.2 0.0 copy-start
  7.2 0.0 all-gather.6.cloned.1.call-start
  7.2 1.5 copy-done
  8.8 5.9 fusion.9
  14.7 0.0 all-gather.6.cloned.1.call-update
  14.7 0.0 reduce-scatter.2.cloned.1.call-start
  14.8 291.4 %all-gather.6.cloned.1.call-done = f32[8192,1024]{1,0:T(8,128)} async-done(((f32[1024,1024]{1,0:T(8,128)}), f32[8192,1024]{1,0:T(8,128)}) %all-gather.6.cloned.1.call-update) | async-done | bytes 33554448 | tf_op jit(solution)/shard_map/all_gather | solution.py:20
  306.2 12.9 %reduce_sum.9 = bf16[1024,1024]{1,0:T(8,128)(2,1)S(1)} reduce(f32[8,1024,1024]{2,1,0:T(8,128)} %bitcast.6, f32[]{:T(128)} %constant.8.clone.1), dimensions={0}, to_apply=%region_2.3 | reduce | flops 7340032 | bytes 35651588 | tf_op jit(solution)/shard_map/reduce_sum | solution.py:20
  319.1 13.0 %convolution_convert_fusion = bf16[1024,3584]{1,0:T(8,128)(2,1)} fusion(bf16[1024,3584]{1,0:T(8,128)(2,1)} %param.7, bf16[1024,1024]{1,0:T(8,128)(2,1)S(1)} %reduce_sum.9), kind=kOutput, calls=%fused_computation.1 | convolution fusion | flops 7519862784 | bytes 16777216 | tf_op jit(solution)/shard_map/dot_general | solution.py:23
  332.1 0.0 copy-start.2
  332.1 0.0 reduce-scatter.2.cloned.1.call-update
  332.1 0.0 all-reduce.3.cloned.1.call-start
  332.1 1.5 copy-done.2
  333.7 2.3 broadcast_select_fusion.1
  336.0 0.0 all-reduce.3.cloned.1.call-update
  336.0 0.2 all-gather.4.cloned.1.call-start
  336.2 73.0 %reduce-scatter.2.cloned.1.call-done = bf16[256,3584]{1,0:T(8,128)(2,1)} async-done(((bf16[1024,3584]{1,0:T(8,128)(2,1)}), bf16[256,3584]{1,0:T(8,128)(2,1)}) %reduce-scatter.2.cloned.1.call-update) | async-done | bytes 1835024 | tf_op jit(solution)/shard_map/reduce_scatter | solution.py:22
  409.2 8.8 %divide_convert_fusion = (bf16[256,3584]{1,0:T(8,128)(2,1)}, f32[256,3584]{1,0:T(8,128)}, f32[256,3584]{1,0:T(8,128)}) fusion(bf16[256,3584]{1,0:T(8,128)(2,1)} %reduce-scatter.2.cloned.1.call-done, f32[256,3584]{1,0:T(8,128)} %param.11, f32[256,3584]{1,0:T(8,128)} %param.10), kind=kLoop, calls=%fused_computation.9 | loop fusion | flops 11010048 | bytes 18350080 | tf_op jit(solution)/shard_map/convert_element_type | solution.py:34
  417.9 0.0 all-gather.4.cloned.1.call-update
  418.0 90.2 %all-reduce.3.cloned.1.call-done = (bf16[1024,1024]{1,0:T(8,128)(2,1)}, bf16[1024,1024]{1,0:T(8,128)(2,1)}) async-done(((bf16[1024,1024]{1,0:T(8,128)(2,1)}, bf16[1024,1024]{1,0:T(8,128)(2,1)}), (bf16[1024,1024]{1,0:T(8,128)(2,1)}, bf16[1024,1024]{1,0:T(8,128)(2,1)})) %all-reduce.3.cloned.1.call-update) | async-done | bytes 4194320 | tf_op jit(solution)/shard_map/psum | solution.py:15
  508.1 81.1 %all-gather.4.cloned.1.call-done = bf16[1024,3584]{1,0:T(8,128)(2,1)} async-done(((bf16[256,3584]{1,0:T(8,128)(2,1)}), bf16[1024,3584]{1,0:T(8,128)(2,1)}) %all-gather.4.cloned.1.call-update) | async-done | bytes 7340048 | tf_op jit(solution)/shard_map/all_gather | solution.py:42
  589.2 0.0 copy-start.1
  589.2 24.2 %subtract_convert_fusion = bf16[2048,3584]{1,0:T(8,128)(2,1)} fusion(bf16[2048,3584]{1,0:T(8,128)(2,1)} %param.9, bf16[1024,3584]{1,0:T(8,128)(2,1)} %all-gather.4.cloned.1.call-done, bf16[1024,1024]{1,0:T(8,128)(2,1)} %get-tuple-element.3, bf16[1024,1024]{1,0:T(8,128)(2,1)} %get-tuple-element.4), kind=kOutput, calls=%fused_computation | convolution fusion | flops 15062794240 | bytes 40894464 | tf_op jit(solution)/shard_map/dot_general | solution.py:44
  613.5 0.0 copy-done.1
Async XLA Ops:
  7.2 1.6 copy-start
  7.2 299.0 %all-gather.6.cloned.1.call-start = ((), (), s32[]{:S(2)}) async-start(), calls=%async_computation.3 | async-start | bytes 37748736 | tf_op jit(solution)/shard_map/all_gather | solution.py:20
  14.7 394.5 %reduce-scatter.2.cloned.1.call-start = ((), (), s32[]{:S(2)}) async-start(), calls=%async_computation.1 | async-start | bytes 9175040 | tf_op jit(solution)/shard_map/reduce_scatter | solution.py:22
  332.1 1.6 copy-start.2
  332.1 176.0 %all-reduce.3.cloned.1.call-start = ((), (), s32[]{:S(2)}) async-start(), calls=%async_computation.4 | async-start | bytes 8388608 | tf_op jit(solution)/shard_map/psum | solution.py:15
  336.0 253.2 %all-gather.4.cloned.1.call-start = ((), (), s32[]{:S(2)}) async-start(), calls=%async_computation.2 | async-start | bytes 9175040 | tf_op jit(solution)/shard_map/all_gather | solution.py:42
  589.2 24.2 %copy-start.1 = (bf16[1024,1024]{1,0:T(8,128)(2,1)S(1)}, bf16[1024,1024]{1,0:T(8,128)(2,1)}, u32[]{:S(2)}) copy-start(bf16[1024,1024]{1,0:T(8,128)(2,1)} %param.6) | copy-start | bytes 6291460
Sparse Core Ops, SparseCore 0:
  14.8 291.3 all-gather.5
  332.2 76.9 reduce-scatter.1
  411.6 96.4 all-reduce.2
  510.4 78.7 all-gather.3
